TPU v7x, 32 devices: a whole 2x2x4 slice. The times are simulated.
32 devices in a mesh: grp: 4 (over x, core), tp: 4 (over z), cores: 2 (over y).
Axes of the slice: x: 2, y: 2, z: 4, core: 2. Of those that a mesh axis runs over, the one named last changes fastest.
Arguments:
- tokens: bfloat16 [4096, 8192], P('grp', ('tp', 'cores')), may hold values from -6 to 6
- gate_up_weight: bfloat16 [8192, 2, 16384], P(None, None, ('tp', 'cores')), may hold values from -0.0625 to 0.0625
- down_factor_pool: bfloat16 [8, 8192, 256], P(('tp', 'cores'), 'grp'), may hold values from -0.0625 to 0.0625
- up_factor_pool: bfloat16 [8, 4, 8, 128, 1024], P(('tp', 'cores'), 'grp'), may hold values from -0.5 to 0.5
- segment_adapters: int32 [4, 3], replicated, may hold values from 0 to 7
- segment_tile_counts: int32 [4, 3], P('grp'), may hold values from 1 to 4, 8 in all within a row
- adapter_pool_rows: int32 [8], replicated, may hold values from 0 to 7, each once
Outputs:
- hidden: bfloat16 [4096, 16384], P('grp', ('tp', 'cores'))
Inputs may be any that keep to these rules, and one draw needn't show every extreme that they name: `segment_tile_counts`: each row sums to 8. `adapter_pool_rows`: each pool row appears once.
All inputs are finite; a program needn't handle non-finite values.
Results may differ from a plain program's by a relative error of at most 0.0036.
Values may be sent and summed in bfloat16 or wider, within the bound.
A program may use at most 320 MiB of HBM per device.

v0:
```python
import jax
import jax.numpy as jnp
from jax import lax
from jax.sharding import PartitionSpec as P

TILE = 128
adapter_scale = 0.5


def tile_segments(tile_lengths, tile_count):
    bounds = jnp.cumsum(tile_lengths)
    positions = jnp.arange(tile_count, dtype=jnp.int32)
    return jnp.sum((bounds[None, :] <= positions[:, None]).astype(jnp.int32), axis=1)


def per_device(
    tokens,
    gate_up_weight,
    down_factor_pool,
    up_factor_pool,
    segment_adapters,
    segment_tile_counts,
    adapter_pool_rows,
):
    groups = lax.axis_size("grp")
    device_shares = lax.axis_size(("tp", "cores"))
    piece_index = lax.axis_index(("tp", "cores"))
    token_count = tokens.shape[0]
    full_width = tokens.shape[1] * device_shares
    local_hidden_width = gate_up_weight.shape[2]
    twice_rank = down_factor_pool.shape[2]
    rank_size = twice_rank // 2
    share_rows = down_factor_pool.shape[1] // device_shares
    local_count = down_factor_pool.shape[0]
    seg_count = segment_adapters.shape[1]
    narrow = local_hidden_width // groups
    local_down_factor = down_factor_pool.reshape(
        local_count, device_shares, share_rows * twice_rank
    )
    local_up_factor = up_factor_pool.reshape(local_count, device_shares, -1)
    a_spread, b_spread = (
        lax.all_to_all(local_down_factor, ("tp", "cores"), split_axis=1, concat_axis=0, tiled=True),
        lax.all_to_all(local_up_factor, ("tp", "cores"), split_axis=1, concat_axis=0, tiled=True),
    )
    all_slots = jnp.take(adapter_pool_rows, segment_adapters)
    a_wanted = jnp.take(a_spread, all_slots, axis=0)
    b_wanted = jnp.take(b_spread, all_slots, axis=0)
    a_arrived, b_arrived = (
        lax.all_to_all(a_wanted, "grp", split_axis=0, concat_axis=2, tiled=True),
        lax.all_to_all(b_wanted, "grp", split_axis=0, concat_axis=2, tiled=True),
    )
    a_chosen = a_arrived.reshape(seg_count, groups, -1)
    b_chosen = b_arrived.reshape(seg_count, groups, -1)
    gathered = lax.all_gather(tokens, ("tp", "cores"), axis=1, tiled=True)
    frozen_output = jnp.dot(
        gathered,
        gate_up_weight.reshape(full_width, 2 * local_hidden_width),
        preferred_element_type=jnp.float32,
    )
    frozen_output = frozen_output.reshape(token_count, 2, local_hidden_width)
    tile_count = token_count // TILE
    tile_seg = tile_segments(segment_tile_counts[0], tile_count)
    a_tiles = jnp.take(a_chosen, tile_seg, axis=0).reshape(
        tile_count, groups * share_rows, twice_rank
    )
    own_features = lax.dynamic_slice_in_dim(
        gathered.reshape(token_count, groups, device_shares, share_rows), piece_index, 1, axis=2
    )
    own_features = own_features.reshape(tile_count, TILE, groups * share_rows)
    partial_shrink = jnp.einsum(
        "tkd,tdr->tkr", own_features, a_tiles, preferred_element_type=jnp.float32
    )
    reduced_input = lax.psum(partial_shrink, ("tp", "cores")).astype(jnp.bfloat16)
    b_tiles = jnp.take(b_chosen, tile_seg, axis=0).reshape(tile_count, groups, rank_size, 2, narrow)
    gate_adapter_delta = jnp.einsum(
        "tkr,tmrw->tkmw",
        reduced_input[:, :, :rank_size],
        b_tiles[:, :, :, 0, :],
        preferred_element_type=jnp.float32,
    )
    up_adapter_delta = jnp.einsum(
        "tkr,tmrw->tkmw",
        reduced_input[:, :, rank_size:],
        b_tiles[:, :, :, 1, :],
        preferred_element_type=jnp.float32,
    )
    gate_combined = frozen_output[:, 0, :] + adapter_scale * gate_adapter_delta.reshape(
        token_count, local_hidden_width
    )
    up_combined = frozen_output[:, 1, :] + adapter_scale * up_adapter_delta.reshape(
        token_count, local_hidden_width
    )
    return (jax.nn.silu(gate_combined) * up_combined).astype(jnp.bfloat16)


def solution(mesh):
    return jax.shard_map(
        per_device,
        mesh=mesh,
        in_specs=(
            P("grp", ("tp", "cores")),
            P(None, None, ("tp", "cores")),
            P(("tp", "cores"), "grp", None),
            P(("tp", "cores"), "grp", None, None, None),
            P(),
            P("grp", None),
            P(),
        ),
        out_specs=P("grp", ("tp", "cores")),
        check_vma=False,
    )
```

profile of v0, /device:TPU:0, one launch (start us, length us, event | category | flops | bytes accessed | tf_op | source)
XLA Modules:
  0.0 634.1 jit_solution(12954752661760870075)
XLA Ops:
  11.1 7.3 %reduce.3 = bf16[8,65536]{1,0:T(8,128)(2,1)S(1)} reduce(bf16[8,1,65536]{2,1,0:T(2,128)(2,1)S(1)} %bitcast.106, bf16[]{:T(256)} %broadcast.154), dimensions={1}, to_apply=%bitcast.85.reduce_sub_computation | reduce | bytes 2097154
  20.3 7.5 %all-to-all-start = ((bf16[8,2,32768]{2,1,0:T(2,128)(2,1)}), bf16[8,2,32768]{2,1,0:T(2,128)(2,1)S(1)}, u32[]{:S(2)}, u32[]{:S(2)}) async-start(bf16[8,2,32768]{2,1,0:T(2,128)(2,1)} %reshape.206), calls=%async_computation | async-start | bytes 2097152 | tf_op jit(solution)/shard_map/all_to_all | solution.py:42
  32.9 13.0 %reduce.2 = bf16[8,131072]{1,0:T(8,128)(2,1)S(1)} reduce(bf16[8,1,131072]{2,1,0:T(2,128)(2,1)} %bitcast.100, bf16[]{:T(256)} %broadcast.154), dimensions={1}, to_apply=%bitcast.83.reduce_sub_computation | reduce | bytes 4194306
  58.1 5.8 reshape.207
  77.6 28.9 %all-to-all-done.2 = bf16[8,2,65536]{2,1,0:T(2,128)(2,1)S(1)} async-done(((bf16[8,2,65536]{2,1,0:T(2,128)(2,1)}), bf16[8,2,65536]{2,1,0:T(2,128)(2,1)S(1)}, u32[]{:S(2)}, u32[]{:S(2)}) %all-to-all-start.2) | async-done | bytes 2097184 | tf_op jit(solution)/shard_map/all_to_all | solution.py:43
  131.6 5.8 fusion.8
  143.2 45.1 %copy.69 = bf16[1024,8,2,2048]{3,1,2,0:T(8,128)(2,1)} copy(bf16[1024,8,2,2048]{3,2,1,0:T(2,128)(2,1)} %bitcast.33) | data formatting | bytes 134217728
  188.3 83.4 %copy.48 = bf16[4096,8192]{1,0:T(8,128)(2,1)} copy(bf16[4096,8192]{0,1:T(8,128)(2,1)} %bitcast.1) | data formatting | bytes 134217728 | tf_op jit(solution)/shard_map/dot_general | solution.py:55
  280.3 7.9 %gather.27 = bf16[8,1024,256]{2,1,0:T(8,128)(2,1)} reshape(bf16[8,4,65536]{2,1,0:T(4,128)(2,1)} %gather_fusion.2) | data formatting | bytes 8388608 | tf_op jit(solution)/shard_map/jit(_take)/gather | solution.py:63
  305.4 8.3 %pad_maximum_fusion = bf16[8,4,131072]{2,1,0:T(4,128)(2,1)} fusion(bf16[8,4,65536]{2,1,0:T(4,128)(2,1)} %gather_fusion.6, bf16[8,4,65536]{2,1,0:T(4,128)(2,1)} %gather_fusion.5), kind=kLoop, calls=%fused_computation.15 | loop fusion | flops 16777216 | bytes 16777216
  313.8 12.5 %reshape.201 = bf16[8,4,128,2,512]{4,3,2,1,0:T(2,128)(2,1)} reshape(bf16[8,4,131072]{2,1,0:T(4,128)(2,1)} %pad_maximum_fusion) | data formatting | bytes 16777216 | tf_op jit(solution)/shard_map/jit(_take)/gather | solution.py:74
  326.3 8.2 %copy_select_fusion = bf16[8,4,128,2,512]{4,2,1,0,3:T(8,128)(2,1)} fusion(bf16[8,4,128,2,512]{4,3,2,1,0:T(2,128)(2,1)} %reshape.201, pred[8]{0:T(512)(128)(4,1)S(1)} %compare_and_fusion.1), kind=kLoop, calls=%fused_computation.16 | loop fusion | flops 4194304 | bytes 16777224 | tf_op jit(solution)/shard_map/jit(_take)/select_n | solution.py:74
  334.6 37.6 %all-gather.2.cloned.1.call-done = bf16[1024,8192]{1,0:T(8,128)(2,1)} async-done(((bf16[1024,1024]{1,0:T(8,128)(2,1)}), bf16[1024,8192]{1,0:T(8,128)(2,1)}) %all-gather.2.cloned.1.call-update) | async-done | bytes 16777232 | tf_op jit(solution)/shard_map/all_gather | solution.py:54
  372.2 10.3 %copy.70 = bf16[128,8,32,256]{3,2,1,0:T(8,128)(2,1)S(1)} copy(bf16[128,8,32,256]{3,1,2,0:T(8,128)(2,1)} %bitcast.102) | data formatting | bytes 33554432
  382.4 13.7 %dynamic-slice_reduce_fusion = bf16[1024,4,256]{2,1,0:T(4,128)(2,1)S(1)} fusion(bf16[1024,4,8,256]{3,2,1,0:T(8,128)(2,1)S(1)} %bitcast.98, s32[]{:T(128)S(6)} %select_n.80), kind=kLoop, calls=%fused_computation.27 | loop fusion | bytes 4194308 | tf_op jit(solution)/shard_map/dynamic_slice | solution.py:66
  402.6 70.0 %all-reduce.1 = bf16[8,128,256]{2,1,0:T(8,128)(2,1)S(1)} all-reduce(f32[8,128,256]{2,1,0:T(8,128)S(1)} %fusion.9), channel_id=1, replica_groups=mesh['grp'=4,'tp'=4,'cores'=2] {'tp','cores'}, use_global_device_ids=true, to_apply=%region_2.3 | all-reduce | flops 262144 | bytes 1572864 | tf_op jit(solution)/shard_map/psum | solution.py:73
  472.6 6.6 %broadcast_multiply_fusion.1 = f32[8,128,4,512]{3,1,2,0:T(8,128)} fusion(bf16[8,4,128,2,512]{4,2,1,0,3:T(8,128)(2,1)} %copy_select_fusion, bf16[8,128,256]{2,1,0:T(8,128)(2,1)S(1)} %all-reduce.1), kind=kOutput, calls=%fused_computation.24 | convolution fusion | flops 538968064 | bytes 12845056 | tf_op jit(solution)/shard_map/tkr,tmrw->tkmw/dot_general | solution.py:75
  479.2 6.6 %broadcast_multiply_fusion = f32[8,128,4,512]{3,1,2,0:T(8,128)} fusion(bf16[8,4,128,2,512]{4,2,1,0,3:T(8,128)(2,1)} %copy_select_fusion, bf16[8,128,256]{2,1,0:T(8,128)(2,1)S(1)} %all-reduce.1), kind=kOutput, calls=%fused_computation.23 | convolution fusion | flops 538968064 | bytes 12845056 | tf_op jit(solution)/shard_map/tkr,tmrw->tkmw/dot_general | solution.py:81
  485.8 12.1 %copy.60 = f32[8,128,4,512]{3,2,1,0:T(4,128)} copy(f32[8,128,4,512]{3,1,2,0:T(8,128)} %broadcast_multiply_fusion) | data formatting | bytes 16777216 | tf_op jit(solution)/shard_map/mul | solution.py:90
  497.9 11.1 %copy.72 = f32[128,8,4,512]{3,1,2,0:T(8,128)} copy(f32[128,8,4,512]{3,2,1,0:T(4,128)} %bitcast.94) | data formatting | bytes 16777216
  509.0 12.1 %copy.59 = f32[8,128,4,512]{3,2,1,0:T(4,128)} copy(f32[8,128,4,512]{3,1,2,0:T(8,128)} %broadcast_multiply_fusion.1) | data formatting | bytes 16777216 | tf_op jit(solution)/shard_map/mul | solution.py:87
  521.0 10.8 %copy.71 = f32[128,8,4,512]{3,1,2,0:T(8,128)} copy(f32[128,8,4,512]{3,2,1,0:T(4,128)} %bitcast.95) | data formatting | bytes 16777216
  531.8 80.5 %fusion = f32[1024,2,2048]{2,0,1:T(8,128)} fusion(bf16[2,2048,8192]{2,1,0:T(8,128)(2,1)} %bitcast.2, bf16[1024,8192]{1,0:T(8,128)(2,1)} %all-gather.2.cloned.1.call-done), kind=kOutput, calls=%fused_computation.7 | convolution fusion | flops 68719476736 | bytes 100663296 | tf_op jit(solution)/shard_map/dot_general | solution.py:55
  612.3 14.8 %fusion.4 = bf16[1024,2048]{1,0:T(8,128)(2,1)} fusion(f32[1024,2048]{1,0:T(8,128)} %bitcast.96, f32[1024,2,2048]{2,0,1:T(8,128)} %fusion, f32[1024,2048]{1,0:T(8,128)} %bitcast.97), kind=kLoop, calls=%fused_computation.12 | loop fusion | flops 16777216 | bytes 37748736 | tf_op jit(solution)/shard_map/convert_element_type | solution.py:93
  (57 shorter events, 100.6 us)
Async XLA Ops:
  6.5 21.4 %copy-start = (s32[8]{0:T(128)S(1)}, s32[8]{0:T(128)}, u32[]{:S(2)}) copy-start(s32[8]{0:T(128)} %param.13) | copy-start | bytes 100
  10.5 17.3 %copy-start.4 = (s32[4,3]{1,0:T(4,128)S(1)}, s32[4,3]{1,0:T(4,128)}, u32[]{:S(2)}) copy-start(s32[4,3]{1,0:T(4,128)} %param.11) | copy-start | bytes 148
  18.4 10.4 %copy-start.3 = (bf16[1,1,8,128,1024]{4,3,2,1,0:T(8,128)(2,1)S(1)}, bf16[1,1,8,128,1024]{4,3,2,1,0:T(8,128)(2,1)}, u32[]{:S(2)}) copy-start(bf16[1,1,8,128,1024]{4,3,2,1,0:T(8,128)(2,1)} %param.10) | copy-start | bytes 6291460
  20.3 33.2 %all-to-all-start = ((bf16[8,2,32768]{2,1,0:T(2,128)(2,1)}), bf16[8,2,32768]{2,1,0:T(2,128)(2,1)S(1)}, u32[]{:S(2)}, u32[]{:S(2)}) async-start(bf16[8,2,32768]{2,1,0:T(2,128)(2,1)} %reshape.206), calls=%async_computation | async-start | bytes 2097152 | tf_op jit(solution)/shard_map/all_to_all | solution.py:42
  53.5 1.0 copy-start.2
  54.5 52.0 %all-to-all-start.2 = ((bf16[8,2,65536]{2,1,0:T(2,128)(2,1)}), bf16[8,2,65536]{2,1,0:T(2,128)(2,1)S(1)}, u32[]{:S(2)}, u32[]{:S(2)}) async-start(bf16[8,2,65536]{2,1,0:T(2,128)(2,1)} %reshape.204), calls=%async_computation.2 | async-start | bytes 4194304 | tf_op jit(solution)/shard_map/all_to_all | solution.py:43
  106.5 30.8 %all-to-all-start.1 = ((bf16[4,3,1,65536]{3,1,2,0:T(4,128)(2,1)}), bf16[4,3,1,65536]{3,1,2,0:T(4,128)(2,1)}, u32[]{:S(2)}, u32[]{:S(2)}) async-start(bf16[4,3,1,65536]{3,1,2,0:T(4,128)(2,1)} %select_bitcast_fusion), calls=%async_computation.1 | async-start | bytes 4194304 | tf_op jit(solution)/shard_map/all_to_all | solution.py:49
  137.3 5.7 copy-start.5
  137.3 150.9 %all-to-all-start.3 = ((bf16[4,3,1,131072]{3,1,2,0:T(4,128)(2,1)}), bf16[4,3,1,131072]{3,1,2,0:T(4,128)(2,1)}, u32[]{:S(2)}, u32[]{:S(2)}) async-start(bf16[4,3,1,131072]{3,1,2,0:T(4,128)(2,1)} %fusion.8), calls=%async_computation.3 | async-start | bytes 8388608 | tf_op jit(solution)/shard_map/all_to_all | solution.py:50
  142.3 229.8 %all-gather.2.cloned.1.call-start = ((), (), s32[]{:S(2)}) async-start(), calls=%async_computation.4 | async-start | bytes 18874368 | tf_op jit(solution)/shard_map/all_gather | solution.py:54
  612.3 14.8 %copy-start.1 = (s32[8]{0:T(128)S(1)}, s32[8]{0:T(128)}, u32[]{:S(2)}) copy-start(s32[8]{0:T(128)} %param.13) | copy-start | bytes 100
Sparse Core Ops, SparseCore 0:
  145.3 226.8 all-gather.1
where the time goes:
time: 644 us; the launch traced here: 634 us
  local copies, waits for them, and re-layouts  299 us (46%)
  matrix products  97.5 us (15%)
  waiting for transfers between devices  71.2 us (11%)
  blocking collectives  70 us (11%)
  other arithmetic  61.6 us (10%)
  starting transfers between devices  21.2 us (3%)
  between operations  13.8 us (2%)
    unnamed x23, local copies, waits for them, and re-layouts  101 us
    dot_general x1, local copies, waits for them, and re-layouts, per_device(): jnp.dot(gathered, gate_up_weight.reshape(full_width, 2 * local_hidden_wid...  83.4 us
    dot_general x1, matrix products, per_device(): jnp.dot(gathered, gate_up_weight.reshape(full_width, 2 * local_hidden_wid...  80.5 us
    psum x1, blocking collectives, per_device(): lax.psum(partial_shrink, ('tp', 'cores')).astype(jnp.bfloat16)  70 us
    all_gather x1, waiting for transfers between devices, per_device(): gathered = lax.all_gather(tokens, ('tp', 'cores'), axis=1, tiled=True)  37.6 us
    all_to_all x1, waiting for transfers between devices, per_device(): lax.all_to_all(local_up_factor, ('tp', 'cores'), split_axis=1, concat_axi...  28.9 us
    unnamed x3, other arithmetic  28.6 us
    gather x4, local copies, waits for them, and re-layouts, per_device(): jnp.take(b_chosen, tile_seg, axis=0)  24.6 us
  transfers between devices with their start and end apart: 5, of which 3 were waited for; matrix products, arithmetic and copies ran while one was open for 41% of the time, Pallas kernels for 0%

commit v1 on v0

--- a/solution.py
+++ b/solution.py
@@ -5,6 +5,11 @@
 
 TILE = 128
 adapter_scale = 0.5
+
+
+def axis_by_axis(value, axis_one, axis_two):
+    half = lax.psum(value, axis_one)
+    return lax.psum(half, axis_two)
 
 
 def tile_segments(tile_lengths, tile_count):
@@ -70,7 +75,7 @@
     partial_shrink = jnp.einsum(
         "tkd,tdr->tkr", own_features, a_tiles, preferred_element_type=jnp.float32
     )
-    reduced_input = lax.psum(partial_shrink, ("tp", "cores")).astype(jnp.bfloat16)
+    reduced_input = axis_by_axis(partial_shrink, "cores", "tp").astype(jnp.bfloat16)
     b_tiles = jnp.take(b_chosen, tile_seg, axis=0).reshape(tile_count, groups, rank_size, 2, narrow)
     gate_adapter_delta = jnp.einsum(
         "tkr,tmrw->tkmw",

time: 644 us -> 615 us (0.955)
  blocking collectives: 70 us -> 42.3 us
    psum x1, blocking collectives: 70 us -> 42.3 us  [axis_by_axis(): return lax.psum(half, axis_two)]
    unnamed x23 -> x27, local copies, waits for them, and re-layouts: 101 us -> 102 us
    unnamed x3 -> x4, other arithmetic: 28.6 us -> 28.7 us
  transfers between devices with their start and end apart: 5 -> 6, of which waited for: 3 -> 3; matrix products, arithmetic and copies ran while one was open for 41% -> 56% of each run, Pallas kernels for 0% -> 0%
where the time goes in v1:
time: 615 us; the launch traced here: 606 us
  local copies, waits for them, and re-layouts  299 us (49%)
  matrix products  99.1 us (16%)
  waiting for transfers between devices  70.7 us (11%)
  other arithmetic  59.1 us (10%)
  blocking collectives  42.3 us (7%)
  starting transfers between devices  21.2 us (3%)
  between operations  13.8 us (2%)
    unnamed x27, local copies, waits for them, and re-layouts  102 us
    dot_general x1, local copies, waits for them, and re-layouts, per_device(): jnp.dot(gathered, gate_up_weight.reshape(full_width, 2 * local_hidden_wid...  83.4 us
    dot_general x1, matrix products, per_device(): jnp.dot(gathered, gate_up_weight.reshape(full_width, 2 * local_hidden_wid...  80.9 us
    psum x1, blocking collectives, axis_by_axis(): return lax.psum(half, axis_two)  42.3 us
    all_gather x1, waiting for transfers between devices, per_device(): gathered = lax.all_gather(tokens, ('tp', 'cores'), axis=1, tiled=True)  36.7 us
    all_to_all x1, waiting for transfers between devices, per_device(): lax.all_to_all(local_up_factor, ('tp', 'cores'), split_axis=1, concat_axi...  28.9 us
    unnamed x4, other arithmetic  28.7 us
    gather x4, local copies, waits for them, and re-layouts, per_device(): jnp.take(b_chosen, tile_seg, axis=0)  24.6 us
  transfers between devices with their start and end apart: 6, of which 3 were waited for; matrix products, arithmetic and copies ran while one was open for 56% of the time, Pallas kernels for 0%

profile of v1, /device:TPU:0, one launch (start us, length us, event | category | flops | bytes accessed | tf_op | source)
XLA Modules:
  0.0 605.5 jit_solution(7252636595005820982)
XLA Ops:
  11.1 7.3 %reduce.3 = bf16[8,65536]{1,0:T(8,128)(2,1)S(1)} reduce(bf16[8,1,65536]{2,1,0:T(2,128)(2,1)S(1)} %bitcast.108, bf16[]{:T(256)} %broadcast.154), dimensions={1}, to_apply=%bitcast.85.reduce_sub_computation | reduce | bytes 2097154
  20.2 7.5 %all-to-all-start = ((bf16[8,2,32768]{2,1,0:T(2,128)(2,1)}), bf16[8,2,32768]{2,1,0:T(2,128)(2,1)S(1)}, u32[]{:S(2)}, u32[]{:S(2)}) async-start(bf16[8,2,32768]{2,1,0:T(2,128)(2,1)} %reshape.206), calls=%async_computation | async-start | bytes 2097152 | tf_op jit(solution)/shard_map/all_to_all | solution.py:47
  32.9 13.0 %reduce.2 = bf16[8,131072]{1,0:T(8,128)(2,1)S(1)} reduce(bf16[8,1,131072]{2,1,0:T(2,128)(2,1)} %bitcast.102, bf16[]{:T(256)} %broadcast.154), dimensions={1}, to_apply=%bitcast.83.reduce_sub_computation | reduce | bytes 4194306
  58.1 5.8 reshape.207
  77.6 28.9 %all-to-all-done.2 = bf16[8,2,65536]{2,1,0:T(2,128)(2,1)S(1)} async-done(((bf16[8,2,65536]{2,1,0:T(2,128)(2,1)}), bf16[8,2,65536]{2,1,0:T(2,128)(2,1)S(1)}, u32[]{:S(2)}, u32[]{:S(2)}) %all-to-all-start.2) | async-done | bytes 2097184 | tf_op jit(solution)/shard_map/all_to_all | solution.py:48
  131.5 5.8 fusion.8
  143.7 45.6 %copy.69 = bf16[1024,8,2,2048]{3,1,2,0:T(8,128)(2,1)} copy(bf16[1024,8,2,2048]{3,2,1,0:T(2,128)(2,1)} %bitcast.33) | data formatting | bytes 134217728
  189.3 83.4 %copy.48 = bf16[4096,8192]{1,0:T(8,128)(2,1)} copy(bf16[4096,8192]{0,1:T(8,128)(2,1)} %bitcast.1) | data formatting | bytes 134217728 | tf_op jit(solution)/shard_map/dot_general | solution.py:60
  281.3 7.9 %gather.27 = bf16[8,1024,256]{2,1,0:T(8,128)(2,1)} reshape(bf16[8,4,65536]{2,1,0:T(4,128)(2,1)} %gather_fusion.2) | data formatting | bytes 8388608 | tf_op jit(solution)/shard_map/jit(_take)/gather | solution.py:68
  306.4 8.4 %pad_maximum_fusion = bf16[8,4,131072]{2,1,0:T(4,128)(2,1)} fusion(bf16[8,4,65536]{2,1,0:T(4,128)(2,1)} %gather_fusion.6, bf16[8,4,65536]{2,1,0:T(4,128)(2,1)} %gather_fusion.5), kind=kLoop, calls=%fused_computation.15 | loop fusion | flops 16777216 | bytes 16777216
  314.8 12.6 %reshape.201 = bf16[8,4,128,2,512]{4,3,2,1,0:T(2,128)(2,1)} reshape(bf16[8,4,131072]{2,1,0:T(4,128)(2,1)} %pad_maximum_fusion) | data formatting | bytes 16777216 | tf_op jit(solution)/shard_map/jit(_take)/gather | solution.py:79
  327.4 8.1 %copy_select_fusion = bf16[8,4,128,2,512]{4,2,1,0,3:T(8,128)(2,1)} fusion(bf16[8,4,128,2,512]{4,3,2,1,0:T(2,128)(2,1)} %reshape.201, pred[8]{0:T(512)(128)(4,1)S(1)} %compare_and_fusion.1), kind=kLoop, calls=%fused_computation.16 | loop fusion | flops 4194304 | bytes 16777224 | tf_op jit(solution)/shard_map/jit(_take)/select_n | solution.py:79
  335.4 36.7 %all-gather.2.cloned.1.call-done = bf16[1024,8192]{1,0:T(8,128)(2,1)} async-done(((bf16[1024,1024]{1,0:T(8,128)(2,1)}), bf16[1024,8192]{1,0:T(8,128)(2,1)}) %all-gather.2.cloned.1.call-update) | async-done | bytes 16777232 | tf_op jit(solution)/shard_map/all_gather | solution.py:59
  372.1 10.3 %copy.70 = bf16[128,8,32,256]{3,2,1,0:T(8,128)(2,1)S(1)} copy(bf16[128,8,32,256]{3,1,2,0:T(8,128)(2,1)} %bitcast.104) | data formatting | bytes 33554432
  382.4 13.7 %dynamic-slice_reduce_fusion = bf16[1024,4,256]{2,1,0:T(4,128)(2,1)S(1)} fusion(bf16[1024,4,8,256]{3,2,1,0:T(8,128)(2,1)S(1)} %bitcast.100, s32[]{:T(128)S(6)} %select_n.80), kind=kLoop, calls=%fused_computation.27 | loop fusion | bytes 4194308 | tf_op jit(solution)/shard_map/dynamic_slice | solution.py:71
  403.7 80.9 %fusion = f32[1024,2,2048]{2,0,1:T(8,128)} fusion(bf16[2,2048,8192]{2,1,0:T(8,128)(2,1)} %bitcast.2, bf16[1024,8192]{1,0:T(8,128)(2,1)} %all-gather.2.cloned.1.call-done), kind=kOutput, calls=%fused_computation.7 | convolution fusion | flops 68719476736 | bytes 100663296 | tf_op jit(solution)/shard_map/dot_general | solution.py:60
  484.6 42.3 %all-reduce.4 = bf16[8,128,256]{2,1,0:T(8,128)(2,1)S(1)} all-reduce(f32[8,128,256]{2,1,0:T(8,128)} %all-reduce.3.cloned.1.call-done), channel_id=1, replica_groups=mesh['grp'=4,'tp'=4,'cores'=2] {'tp'}, use_global_device_ids=true, to_apply=%region_3.4 | all-reduce | flops 262144 | bytes 1572864 | tf_op jit(solution)/shard_map/psum | solution.py:12
  526.9 6.7 %broadcast_multiply_fusion.1 = f32[8,128,4,512]{3,1,2,0:T(8,128)} fusion(bf16[8,4,128,2,512]{4,2,1,0,3:T(8,128)(2,1)} %copy_select_fusion, bf16[8,128,256]{2,1,0:T(8,128)(2,1)S(1)} %all-reduce.4), kind=kOutput, calls=%fused_computation.24 | convolution fusion | flops 538968064 | bytes 12845056 | tf_op jit(solution)/shard_map/tkr,tmrw->tkmw/dot_general | solution.py:80
  533.5 6.7 %broadcast_multiply_fusion = f32[8,128,4,512]{3,1,2,0:T(8,128)} fusion(bf16[8,4,128,2,512]{4,2,1,0,3:T(8,128)(2,1)} %copy_select_fusion, bf16[8,128,256]{2,1,0:T(8,128)(2,1)S(1)} %all-reduce.4), kind=kOutput, calls=%fused_computation.23 | convolution fusion | flops 538968064 | bytes 12845056 | tf_op jit(solution)/shard_map/tkr,tmrw->tkmw/dot_general | solution.py:86
  540.2 12.0 %copy.60 = f32[8,128,4,512]{3,2,1,0:T(4,128)} copy(f32[8,128,4,512]{3,1,2,0:T(8,128)} %broadcast_multiply_fusion) | data formatting | bytes 16777216 | tf_op jit(solution)/shard_map/mul | solution.py:95
  552.2 10.9 %copy.72 = f32[128,8,4,512]{3,1,2,0:T(8,128)} copy(f32[128,8,4,512]{3,2,1,0:T(4,128)} %bitcast.94) | data formatting | bytes 16777216
  563.1 12.0 %copy.59 = f32[8,128,4,512]{3,2,1,0:T(4,128)} copy(f32[8,128,4,512]{3,1,2,0:T(8,128)} %broadcast_multiply_fusion.1) | data formatting | bytes 16777216 | tf_op jit(solution)/shard_map/mul | solution.py:92
  575.1 11.0 %copy.71 = f32[128,8,4,512]{3,1,2,0:T(8,128)} copy(f32[128,8,4,512]{3,2,1,0:T(4,128)} %bitcast.95) | data formatting | bytes 16777216
  586.0 12.4 %fusion.4 = bf16[1024,2048]{1,0:T(8,128)(2,1)} fusion(f32[1024,2048]{1,0:T(8,128)S(1)} %bitcast.98, f32[1024,2,2048]{2,0,1:T(8,128)} %fusion, f32[1024,2048]{1,0:T(8,128)} %bitcast.99), kind=kLoop, calls=%fused_computation.12 | loop fusion | flops 16777216 | bytes 37748736 | tf_op jit(solution)/shard_map/convert_element_type | solution.py:98
  (65 shorter events, 102.1 us)
Async XLA Ops:
  6.5 21.3 %copy-start = (s32[8]{0:T(128)S(1)}, s32[8]{0:T(128)}, u32[]{:S(2)}) copy-start(s32[8]{0:T(128)} %param.13) | copy-start | bytes 100
  10.5 17.2 %copy-start.4 = (s32[4,3]{1,0:T(4,128)S(1)}, s32[4,3]{1,0:T(4,128)}, u32[]{:S(2)}) copy-start(s32[4,3]{1,0:T(4,128)} %param.11) | copy-start | bytes 148
  18.4 10.4 %copy-start.3 = (bf16[1,1,8,128,1024]{4,3,2,1,0:T(8,128)(2,1)S(1)}, bf16[1,1,8,128,1024]{4,3,2,1,0:T(8,128)(2,1)}, u32[]{:S(2)}) copy-start(bf16[1,1,8,128,1024]{4,3,2,1,0:T(8,128)(2,1)} %param.10) | copy-start | bytes 6291460
  20.2 33.2 %all-to-all-start = ((bf16[8,2,32768]{2,1,0:T(2,128)(2,1)}), bf16[8,2,32768]{2,1,0:T(2,128)(2,1)S(1)}, u32[]{:S(2)}, u32[]{:S(2)}) async-start(bf16[8,2,32768]{2,1,0:T(2,128)(2,1)} %reshape.206), calls=%async_computation | async-start | bytes 2097152 | tf_op jit(solution)/shard_map/all_to_all | solution.py:47
  53.5 1.0 copy-start.2
  54.5 52.0 %all-to-all-start.2 = ((bf16[8,2,65536]{2,1,0:T(2,128)(2,1)}), bf16[8,2,65536]{2,1,0:T(2,128)(2,1)S(1)}, u32[]{:S(2)}, u32[]{:S(2)}) async-start(bf16[8,2,65536]{2,1,0:T(2,128)(2,1)} %reshape.204), calls=%async_computation.2 | async-start | bytes 4194304 | tf_op jit(solution)/shard_map/all_to_all | solution.py:48
  106.5 30.8 %all-to-all-start.1 = ((bf16[4,3,1,65536]{3,1,2,0:T(4,128)(2,1)}), bf16[4,3,1,65536]{3,1,2,0:T(4,128)(2,1)}, u32[]{:S(2)}, u32[]{:S(2)}) async-start(bf16[4,3,1,65536]{3,1,2,0:T(4,128)(2,1)} %select_bitcast_fusion), calls=%async_computation.1 | async-start | bytes 4194304 | tf_op jit(solution)/shard_map/all_to_all | solution.py:54
  137.3 6.2 %copy-start.5 = (s32[1,3]{1,0:T(1,128)S(1)}, s32[1,3]{1,0:T(1,128)}, u32[]{:S(2)}) copy-start(s32[1,3]{1,0:T(1,128)} %param.12) | copy-start | bytes 40
  137.3 151.9 %all-to-all-start.3 = ((bf16[4,3,1,131072]{3,1,2,0:T(4,128)(2,1)}), bf16[4,3,1,131072]{3,1,2,0:T(4,128)(2,1)}, u32[]{:S(2)}, u32[]{:S(2)}) async-start(bf16[4,3,1,131072]{3,1,2,0:T(4,128)(2,1)} %fusion.8), calls=%async_computation.3 | async-start | bytes 8388608 | tf_op jit(solution)/shard_map/all_to_all | solution.py:55
  142.3 229.8 %all-gather.2.cloned.1.call-start = ((), (), s32[]{:S(2)}) async-start(), calls=%async_computation.4 | async-start | bytes 18874368 | tf_op jit(solution)/shard_map/all_gather | solution.py:59
  143.0 341.5 %all-reduce.3.cloned.1.call-start = ((), (), s32[]{:S(2)}) async-start(), calls=%async_computation.5 | async-start | bytes 2097152 | tf_op jit(solution)/shard_map/psum | solution.py:11
  575.1 11.0 %slice-start = ((s8[8388608]{0:T(1024)(128)(4,1)}), s8[4194304]{0:T(1024)(128)(4,1)S(1)}, s32[]{:S(2)}) async-start(s8[8388608]{0:T(1024)(128)(4,1)} %bitcast.96), calls=%async_computation.6 | async-start | bytes 8388608
  575.1 11.0 %slice-start.1 = ((s8[8388608]{0:T(1024)(128)(4,1)}), s8[4194304]{0:T(1024)(128)(4,1)S(1)}, s32[]{:S(2)}) async-start(s8[8388608]{0:T(1024)(128)(4,1)} %bitcast.96), calls=%async_computation.7 | async-start | bytes 8388608
  586.0 12.4 %copy-start.1 = (s32[8]{0:T(128)S(1)}, s32[8]{0:T(128)}, u32[]{:S(2)}) copy-start(s32[8]{0:T(128)} %param.13) | copy-start | bytes 100
Sparse Core Ops, SparseCore 0:
  145.3 226.7 all-gather.1
  403.8 38.2 all-reduce.2
